TPU v7x, 32 devices: a whole 2x2x4 slice. The times are simulated.
32 devices in a mesh: groups: 2 (over x), ep: 16 (over z, y, core).
Axes of the slice: x: 2, y: 2, z: 4, core: 2. Of those that a mesh axis runs over, the one named last changes fastest.
Arguments:
- residual: bfloat16 [2048, 7168], P('groups', 'ep'), parts along dimension 0, may hold values from -6 to 6
- attn_out: bfloat16 [2048, 7168], P('groups', 'ep'), parts along dimension 0, may hold values from -6 to 6
- norm_gain: float32 [7168], replicated, may hold values from 0.5 to 1.5
- expert_routes: int32 [2048, 2], P(('groups', 'ep')), parts along dimension 0, may hold values from 0 to 2, as said below
- route_gain: float32 [2048, 2], P(('groups', 'ep')), parts along dimension 0, may hold values from 0.1 to 1
- w_gate: bfloat16 [7168, 4096], P(None, 'ep'), may hold values from -0.0625 to 0.0625
- w_up: bfloat16 [7168, 4096], P(None, 'ep'), may hold values from -0.0625 to 0.0625
- w_down: bfloat16 [4096, 7168], P('ep'), may hold values from -0.125 to 0.125
Outputs:
- mixed: bfloat16 [2048, 7168], P(('groups', 'ep')), parts along dimension 0
There are 2 independent parts, one for each index of `groups`. A program takes and returns all parts, laid end to end along the dimension named above; an argument that names none is the same for every part. Nothing has to cross between parts.
Inputs may be any that keep to these rules, and one draw needn't show every extreme that they name: `expert_routes`: value 2 marks a route to an expert outside this wave; a token names each expert of the wave at most once. Among the tokens of one block of 64, at most 64 routes name one expert, and in every draw some expert is named exactly 64 times by every block.
All inputs are finite; a program needn't handle non-finite values.
Results may differ from a plain program's by a relative error of at most 0.0055.
Values may be sent and summed in bfloat16 or wider, within the bound.
A program may use at most 192 MiB of HBM per device.

v0:
```python
import jax
import jax.numpy as jnp
from jax import lax
from jax.sharding import PartitionSpec as P

FSPLIT = 8
epsilon = 1e-06


def normalize(stream_rows, norm_gain):
    values = stream_rows.astype(jnp.float32)
    inv_rms = lax.rsqrt(jnp.mean(values * values, axis=-1, keepdims=True) + epsilon)
    return (values * inv_rms * norm_gain).astype(jnp.bfloat16)


def route_match(routes, experts, capacity):
    flat_ids = routes.reshape(-1)
    onehot = (flat_ids[:, None] == jnp.arange(experts, dtype=jnp.int32)[None, :]).astype(jnp.int32)
    earlier = jnp.cumsum(onehot, axis=0) - onehot
    slot_pos = jnp.sum(earlier * onehot, axis=1)
    slot_code = jnp.where(flat_ids < experts, flat_ids * capacity + slot_pos, -1)
    target = jnp.arange(experts * capacity, dtype=jnp.int32)
    return slot_code[None, :] == target[:, None]


def selection(routes, experts, capacity):
    matched = route_match(routes, experts, capacity).astype(jnp.int32)
    return matched.reshape(experts * capacity, routes.shape[0], routes.shape[1]).sum(axis=2)


def gain_table(routes, route_gain, experts, capacity):
    matched = route_match(routes, experts, capacity)
    weighted = jnp.where(matched, route_gain.reshape(-1)[None, :], 0.0)
    return weighted.reshape(experts * capacity, routes.shape[0], routes.shape[1]).sum(axis=2).T


def expert_rows(normed, w_gate, w_up, w_down):
    gate_act = jnp.dot(normed, w_gate, preferred_element_type=jnp.float32)
    up_act = jnp.dot(normed, w_up, preferred_element_type=jnp.float32)
    hidden = (jax.nn.silu(gate_act) * up_act).astype(jnp.bfloat16)
    return jnp.dot(hidden, w_down, preferred_element_type=jnp.float32).astype(jnp.bfloat16)


def body(residual, attn_out, norm_gain, expert_routes, route_gain, w_gate, w_up, w_down):
    devices = lax.axis_size("ep")
    tok_here = expert_routes.shape[0]
    route_slots = expert_routes.shape[1]
    experts = devices // FSPLIT
    capacity = route_slots * tok_here // experts
    model_width = w_gate.shape[0]
    stream_feat = (residual.astype(jnp.float32) + attn_out.astype(jnp.float32)).astype(jnp.bfloat16)
    stream_rows = lax.all_to_all(stream_feat, "ep", split_axis=0, concat_axis=1, tiled=True)
    combine_weights = gain_table(expert_routes, route_gain, experts, capacity)
    normed_rows = normalize(stream_rows, norm_gain)
    select = selection(expert_routes, experts, capacity).astype(jnp.bfloat16)
    per_expert = jnp.dot(select, normed_rows, preferred_element_type=jnp.float32).astype(
        jnp.bfloat16
    )
    per_expert = per_expert.reshape(experts, 1, capacity, model_width)
    outgoing = jnp.broadcast_to(per_expert, (experts, FSPLIT, capacity, model_width))
    outgoing = outgoing.reshape(devices, capacity, model_width)
    received = lax.all_to_all(outgoing, "ep", split_axis=0, concat_axis=0, tiled=True)
    slot_count = received.shape[1]
    partial_value = expert_rows(received.reshape(-1, model_width), w_gate, w_up, w_down)
    partial_value = partial_value.reshape(devices, slot_count, model_width)
    returned = lax.all_to_all(partial_value, "ep", split_axis=0, concat_axis=0, tiled=True)
    summed = (
        returned.reshape(experts, FSPLIT, capacity, model_width).astype(jnp.float32).sum(axis=1)
    )
    summed = summed.reshape(experts * capacity, model_width)
    routed_sum = jnp.dot(combine_weights, summed, precision=lax.Precision.HIGHEST)
    return (stream_rows.astype(jnp.float32) + routed_sum).astype(jnp.bfloat16)


def dense_body(residual, attn_out, norm_gain, expert_routes, route_gain, w_gate, w_up, w_down):
    devices = lax.axis_size("ep")
    rank = lax.axis_index("ep")
    tok_here = expert_routes.shape[0]
    experts = devices // FSPLIT
    stream_feat = (residual.astype(jnp.float32) + attn_out.astype(jnp.float32)).astype(jnp.bfloat16)
    named = jnp.arange(experts, dtype=jnp.int32)
    gains = jnp.sum(
        jnp.where(expert_routes[:, :, None] == named, route_gain[:, :, None], 0.0), axis=1
    )
    all_gains = lax.all_gather(gains, "ep", axis=0, tiled=True)
    here = (rank // FSPLIT == named).astype(jnp.float32)
    gain_here = jnp.sum(all_gains * here, axis=1, keepdims=True)
    stream = lax.all_gather(stream_feat, "ep", axis=1, tiled=True)
    normed = normalize(stream, norm_gain)
    gate_act = jnp.dot(normed, w_gate, preferred_element_type=jnp.float32)
    up_act = jnp.dot(normed, w_up, preferred_element_type=jnp.float32)
    hidden = (jax.nn.silu(gate_act) * up_act * gain_here).astype(jnp.bfloat16)
    partial = jnp.dot(hidden, w_down, preferred_element_type=jnp.float32).astype(jnp.bfloat16)
    routed = lax.psum_scatter(partial, "ep", scatter_dimension=0, tiled=True)
    own = lax.dynamic_slice_in_dim(stream, rank * tok_here, tok_here, 0)
    return (own.astype(jnp.float32) + routed.astype(jnp.float32)).astype(jnp.bfloat16)


def pick_body(residual, attn_out, norm_gain, expert_routes, route_gain, w_gate, w_up, w_down):
    experts = lax.axis_size("ep") // FSPLIT
    capacity = expert_routes.shape[1] * expert_routes.shape[0] // experts
    run = dense_body if capacity >= expert_routes.shape[0] else body
    return run(residual, attn_out, norm_gain, expert_routes, route_gain, w_gate, w_up, w_down)


def solution(mesh):
    in_specs = (
        P("groups", "ep"),
        P("groups", "ep"),
        P(),
        P(("groups", "ep"), None),
        P(("groups", "ep"), None),
        P(None, "ep"),
        P(None, "ep"),
        P("ep", None),
    )
    out_specs = P(("groups", "ep"), None)
    return jax.shard_map(
        pick_body, mesh=mesh, in_specs=in_specs, out_specs=out_specs, check_vma=False
    )
```

profile of v0, /device:TPU:0, one launch (start us, length us, event | category | flops | bytes accessed | tf_op | source)
XLA Modules:
  0.0 322.8 jit_solution(7956764136521179954)
XLA Ops:
  6.5 0.0 copy-start.1
  6.5 0.0 all-gather.3.cloned.1.call-start
  6.5 2.7 add_convert_fusion.1
  9.3 0.0 all-gather.3.cloned.1.call-update
  9.3 0.0 reduce-scatter.2.cloned.1.call-start
  9.4 0.7 fusion.23
  10.1 23.6 %all-gather = f32[16,64,2]{1,2,0:T(2,128)S(1)} all-gather(f32[1,64,2]{1,2,0:T(2,128)S(1)} %bitcast.11), channel_id=1, replica_groups=mesh['groups'=2,'ep'=16] {'ep'}, dimensions={0}, use_global_device_ids=true | all-gather | bytes 8704 | tf_op jit(solution)/shard_map/all_gather | solution.py:85
  33.7 0.1 reshape.18
  33.8 0.1 multiply_reduce_fusion
  33.9 91.9 %all-gather.3.cloned.1.call-done = bf16[1024,7168]{0,1:T(8,128)(2,1)} async-done(((bf16[1024,448]{0,1:T(8,128)(2,1)}), bf16[1024,7168]{0,1:T(8,128)(2,1)}) %all-gather.3.cloned.1.call-update) | async-done | bytes 14680080 | tf_op jit(solution)/shard_map/all_gather | solution.py:88
  125.8 8.1 %fusion = f32[1024]{0:T(1024)S(1)} fusion(bf16[1024,7168]{0,1:T(8,128)(2,1)} %all-gather.3.cloned.1.call-done), kind=kLoop, calls=%fused_computation.2 | loop fusion | flops 22019072 | bytes 14684160 | tf_op jit(solution)/shard_map/reduce_sum | solution.py:12
  133.8 0.0 copy-done.1
  133.9 0.0 copy-start
  133.9 12.8 %fusion.5 = f32[1024,256]{1,0:T(8,128)} fusion(bf16[7168,256]{1,0:T(8,128)(2,1)} %param.13, bf16[1024,7168]{0,1:T(8,128)(2,1)} %all-gather.3.cloned.1.call-done, f32[7168]{0:T(1024)S(1)} %copy-done.1, f32[1024]{0:T(1024)S(1)} %add_rsqrt_fusion), kind=kOutput, calls=%fused_computation.7 | convolution fusion | flops 3787456512 | bytes 19431424 | tf_op jit(solution)/shard_map/dot_general | solution.py:90
  146.6 0.0 copy-done
  146.6 9.2 %fusion.13.clone.4 = bf16[1024,256]{1,0:T(8,128)(2,1)S(1)} fusion(bf16[7168,256]{1,0:T(8,128)(2,1)} %param.14, bf16[1024,7168]{0,1:T(8,128)(2,1)S(1)} %copy-done, f32[7168]{0:T(1024)S(1)} %copy-done.1, f32[1024]{0:T(1024)S(1)} %add_rsqrt_fusion, f32[1024,256]{1,0:T(8,128)} %fusion.5, f32[1024]{0:T(1024)S(1)} %multiply_reduce_fusion), kind=kOutput, calls=%fused_computation.12.clone.clone.clone.1 | convolution fusion | flops 3789291520 | bytes 19959808 | tf_op jit(solution)/shard_map/dot_general | solution.py:91
  155.8 9.3 %convolution_convert_fusion = bf16[1024,7168]{1,0:T(8,128)(2,1)} fusion(bf16[256,7168]{1,0:T(8,128)(2,1)} %param.15, bf16[1024,256]{1,0:T(8,128)(2,1)S(1)} %fusion.13.clone.4), kind=kOutput, calls=%fused_computation.5 | convolution fusion | flops 3765436416 | bytes 18874368 | tf_op jit(solution)/shard_map/dot_general | solution.py:93
  165.1 0.0 reduce-scatter.2.cloned.1.call-update
  165.2 2.1 constant_dynamic-slice_fusion
  167.2 0.8 copy.24
  168.0 145.6 %reduce-scatter.2.cloned.1.call-done = bf16[64,7168]{1,0:T(8,128)(2,1)} async-done(((bf16[1024,7168]{1,0:T(8,128)(2,1)}), bf16[64,7168]{1,0:T(8,128)(2,1)}) %reduce-scatter.2.cloned.1.call-update) | async-done | bytes 917520 | tf_op jit(solution)/shard_map/reduce_scatter | solution.py:94
  313.6 2.3 add_convert_fusion
  (3 shorter events, 0.0 us)
Async XLA Ops:
  6.5 127.3 %copy-start.1 = (f32[7168]{0:T(1024)S(1)}, f32[7168]{0:T(1024)}, u32[]{:S(2)}) copy-start(f32[7168]{0:T(1024)} %param.10) | copy-start | bytes 86020
  6.5 119.2 %all-gather.3.cloned.1.call-start = ((), (), s32[]{:S(2)}) async-start(), calls=%async_computation.1 | async-start | bytes 15597568 | tf_op jit(solution)/shard_map/all_gather | solution.py:88
  9.3 304.3 %reduce-scatter.2.cloned.1.call-start = ((), (), s32[]{:S(2)}) async-start(), calls=%async_computation.2 | async-start | bytes 15597568 | tf_op jit(solution)/shard_map/reduce_scatter | solution.py:94
  133.9 12.8 %copy-start = (bf16[1024,7168]{0,1:T(8,128)(2,1)S(1)}, bf16[1024,7168]{0,1:T(8,128)(2,1)}, u32[]{:S(2)}) copy-start(bf16[1024,7168]{0,1:T(8,128)(2,1)} %all-gather.3.cloned.1.call-done) | copy-start | bytes 44040196
Sparse Core Ops, SparseCore 0:
  9.6 116.0 all-gather.2
  165.3 148.2 reduce-scatter.1
where the time goes:
time: 323 us
  waiting for transfers between devices  238 us (74%)
  matrix products  31.3 us (10%)
  blocking collectives  23.6 us (7%)
  other arithmetic  13.9 us (4%)
  between operations  13.5 us (4%)
    reduce_scatter x1, waiting for transfers between devices, dense_body(): routed = lax.psum_scatter(partial, 'ep', scatter_dimension=0, tiled=True)  146 us
    all_gather x1, waiting for transfers between devices, dense_body(): stream = lax.all_gather(stream_feat, 'ep', axis=1, tiled=True)  91.9 us
    all_gather x1, blocking collectives, dense_body(): all_gains = lax.all_gather(gains, 'ep', axis=0, tiled=True)  23.6 us
    dot_general x1, matrix products, dense_body(): gate_act = jnp.dot(normed, w_gate, preferred_element_type=jnp.float32)  12.8 us
    dot_general x1, matrix products, dense_body(): jnp.dot(hidden, w_down, preferred_element_type=jnp.float32)  9.34 us
    dot_general x1, matrix products, dense_body(): up_act = jnp.dot(normed, w_up, preferred_element_type=jnp.float32)  9.16 us
    reduce_sum x1, other arithmetic, normalize(): jnp.mean(values * values, axis=-1, keepdims=True) + epsilon  8.08 us
  transfers between devices with their start and end apart: 2, of which 2 were waited for; matrix products, arithmetic and copies ran while one was open for 1% of the time, Pallas kernels for 0%

commit v1 on v0

--- a/solution.py
+++ b/solution.py
@@ -85,7 +85,10 @@
     all_gains = lax.all_gather(gains, "ep", axis=0, tiled=True)
     here = (rank // FSPLIT == named).astype(jnp.float32)
     gain_here = jnp.sum(all_gains * here, axis=1, keepdims=True)
-    stream = lax.all_gather(stream_feat, "ep", axis=1, tiled=True)
+    peers = lax.axis_size("ep")
+    blocks = jnp.stack([stream_feat for _ in range(peers)])
+    blocks = lax.all_to_all(blocks, "ep", split_axis=0, concat_axis=0)
+    stream = jnp.concatenate(blocks, axis=1)
     normed = normalize(stream, norm_gain)
     gate_act = jnp.dot(normed, w_gate, preferred_element_type=jnp.float32)
     up_act = jnp.dot(normed, w_up, preferred_element_type=jnp.float32)

time: 323 us -> 548 us (1.70)
  blocking collectives: 23.6 us -> 252 us
  waiting for transfers between devices: 238 us -> 222 us
  starting transfers between devices: 0.04 us -> 7.63 us
  local copies, waits for them, and re-layouts: 2.91 us -> 10 us
    all_gather x1, blocking collectives: 23.6 us -> 252 us  [dense_body(): all_gains = lax.all_gather(gains, 'ep', axis=0, tiled=True)]
    all_gather x1 -> x0, waiting for transfers between devices: 91.9 us -> none  [dense_body(): stream = lax.all_gather(stream_feat, 'ep', axis=1, tiled=True)]
    reduce_scatter x1, waiting for transfers between devices: 146 us -> 214 us  [dense_body(): routed = lax.psum_scatter(partial, 'ep', scatter_dimension=0, tiled=True)]
    all_to_all x0 -> x1, starting transfers between devices: none -> 7.59 us  [dense_body(): blocks = lax.all_to_all(blocks, 'ep', split_axis=0, concat_axis=0)]
    all_to_all x0 -> x1, waiting for transfers between devices: none -> 7.49 us  [dense_body(): blocks = lax.all_to_all(blocks, 'ep', split_axis=0, concat_axis=0)]
    another operation x0 -> x1, local copies, waits for them, and re-layouts: none -> 7.09 us  [dense_body(): blocks = jnp.stack([stream_feat for _ in range(peers)])]
where the time goes in v1:
time: 548 us; the launch traced here: 547 us
  blocking collectives  252 us (46%)
  waiting for transfers between devices  222 us (41%)
  matrix products  29.6 us (5%)
  between operations  13.5 us (2%)
  other arithmetic  12.3 us (2%)
  local copies, waits for them, and re-layouts  10 us (2%)
  starting transfers between devices  7.63 us (1%)
    all_gather x1, blocking collectives, dense_body(): all_gains = lax.all_gather(gains, 'ep', axis=0, tiled=True)  252 us
    reduce_scatter x1, waiting for transfers between devices, dense_body(): routed = lax.psum_scatter(partial, 'ep', scatter_dimension=0, tiled=True)  214 us
    dot_general x1, matrix products, dense_body(): gate_act = jnp.dot(normed, w_gate, preferred_element_type=jnp.float32)  11.8 us
  transfers between devices with their start and end apart: 2, of which 2 were waited for; matrix products, arithmetic and copies ran while one was open for 1% of the time, Pallas kernels for 0%

profile of v1, /device:TPU:0, one launch (start us, length us, event | category | flops | bytes accessed | tf_op | source)
XLA Modules:
  0.0 547.2 jit_solution(7529189466386126376)
XLA Ops:
  6.5 1.8 add_convert_fusion.1
  8.3 7.1 %stack.2 = bf16[16,1024,448]{1,2,0:T(8,128)(2,1)} broadcast(bf16[1024,448]{0,1:T(8,128)(2,1)S(1)} %add_convert_fusion.1), dimensions={1,2} | broadcast | bytes 15597568 | tf_op jit(solution)/shard_map/stack | solution.py:89
  15.4 0.0 copy-start.1
  15.4 0.0 copy-start.2
  15.4 7.6 %all-to-all-start = ((bf16[16,1024,448]{1,2,0:T(8,128)(2,1)}), bf16[16,1024,448]{1,2,0:T(8,128)(2,1)}, u32[]{:S(2)}, u32[]{:S(2)}) async-start(bf16[16,1024,448]{1,2,0:T(8,128)(2,1)} %stack.2), calls=%async_computation | async-start | bytes 29360128 | tf_op jit(solution)/shard_map/all_to_all | solution.py:90
  23.0 0.0 copy-start.4
  23.0 0.0 reduce-scatter.2.cloned.1.call-start
  23.1 0.0 copy-done.1
  23.1 0.0 copy-done.2
  23.1 252.5 %all-gather = f32[16,64,2]{1,2,0:T(2,128)S(1)} all-gather(f32[1,64,2]{1,2,0:T(2,128)S(1)} %bitcast.15), channel_id=1, replica_groups=mesh['groups'=2,'ep'=16] {'ep'}, dimensions={0}, use_global_device_ids=true | all-gather | bytes 8704 | tf_op jit(solution)/shard_map/all_gather | solution.py:85
  275.6 0.1 reshape.28
  275.7 0.1 multiply_reduce_fusion.1
  275.8 7.5 %all-to-all-done = bf16[16,1024,448]{1,2,0:T(8,128)(2,1)} async-done(((bf16[16,1024,448]{1,2,0:T(8,128)(2,1)}), bf16[16,1024,448]{1,2,0:T(8,128)(2,1)}, u32[]{:S(2)}, u32[]{:S(2)}) %all-to-all-start) | async-done | bytes 14680096 | tf_op jit(solution)/shard_map/all_to_all | solution.py:90
  283.3 8.1 %multiply_reduce_fusion = f32[1024]{0:T(1024)S(1)} fusion(bf16[16,1024,448]{1,2,0:T(8,128)(2,1)} %all-to-all-done), kind=kLoop, calls=%fused_computation.1 | loop fusion | flops 22019072 | bytes 14684160 | tf_op jit(solution)/shard_map/reduce_sum | solution.py:12
  291.4 0.0 copy-done.4
  291.4 0.0 copy-start.3
  291.4 11.8 %fusion.1 = f32[1024,256]{1,0:T(8,128)S(1)} fusion(bf16[7168,256]{1,0:T(8,128)(2,1)} %param.13, bf16[1024,7168]{0,1:T(8,128)(2,1)} %bitcast.1, f32[7168]{0:T(1024)S(1)} %copy-done.4, f32[1024]{0:T(1024)S(1)} %add_rsqrt_fusion), kind=kOutput, calls=%fused_computation.4 | convolution fusion | flops 3787456512 | bytes 19431424 | tf_op jit(solution)/shard_map/dot_general | solution.py:93
  303.1 0.0 copy-done.3
  303.2 0.0 copy-start
  303.2 10.6 %fusion.4.clone.4 = bf16[1024,256]{1,0:T(8,128)(2,1)S(1)} fusion(bf16[7168,256]{1,0:T(8,128)(2,1)S(1)} %copy-done.3, bf16[1024,7168]{0,1:T(8,128)(2,1)} %bitcast.1, f32[7168]{0:T(1024)S(1)} %copy-done.4, f32[1024]{0:T(1024)S(1)} %add_rsqrt_fusion, f32[1024,256]{1,0:T(8,128)S(1)} %fusion.1, f32[1024]{0:T(1024)S(1)} %multiply_reduce_fusion.1), kind=kOutput, calls=%fused_computation.9.clone.clone.clone.1 | convolution fusion | flops 3789291520 | bytes 19959808 | tf_op jit(solution)/shard_map/dot_general | solution.py:94
  313.8 0.0 copy-done
  313.8 7.3 %convolution_convert_fusion = bf16[1024,7168]{1,0:T(8,128)(2,1)} fusion(bf16[256,7168]{1,0:T(8,128)(2,1)S(1)} %copy-done, bf16[1024,256]{1,0:T(8,128)(2,1)S(1)} %fusion.4.clone.4), kind=kOutput, calls=%fused_computation.2 | convolution fusion | flops 3765436416 | bytes 18874368 | tf_op jit(solution)/shard_map/dot_general | solution.py:96
  321.1 0.0 reduce-scatter.2.cloned.1.call-update
  321.1 2.1 constant_dynamic-slice_fusion
  323.2 0.8 copy.22
  323.9 214.1 %reduce-scatter.2.cloned.1.call-done = bf16[64,7168]{1,0:T(8,128)(2,1)} async-done(((bf16[1024,7168]{1,0:T(8,128)(2,1)}), bf16[64,7168]{1,0:T(8,128)(2,1)}) %reduce-scatter.2.cloned.1.call-update) | async-done | bytes 917520 | tf_op jit(solution)/shard_map/reduce_scatter | solution.py:97
  538.1 2.3 add_convert_fusion
  (4 shorter events, 0.0 us)
Async XLA Ops:
  15.4 7.7 %copy-start.1 = (f32[64,2]{0,1:T(2,128)S(1)}, f32[64,2]{0,1:T(2,128)}, u32[]{:S(2)}) copy-start(f32[64,2]{0,1:T(2,128)} %param.12) | copy-start | bytes 1540
  15.4 7.7 %copy-start.2 = (s32[64,2]{0,1:T(2,128)S(1)}, s32[64,2]{0,1:T(2,128)}, u32[]{:S(2)}) copy-start(s32[64,2]{0,1:T(2,128)} %param.11) | copy-start | bytes 1540
  15.4 267.8 %all-to-all-start = ((bf16[16,1024,448]{1,2,0:T(8,128)(2,1)}), bf16[16,1024,448]{1,2,0:T(8,128)(2,1)}, u32[]{:S(2)}, u32[]{:S(2)}) async-start(bf16[16,1024,448]{1,2,0:T(8,128)(2,1)} %stack.2), calls=%async_computation | async-start | bytes 29360128 | tf_op jit(solution)/shard_map/all_to_all | solution.py:90
  23.0 268.3 %copy-start.4 = (f32[7168]{0:T(1024)S(1)}, f32[7168]{0:T(1024)}, u32[]{:S(2)}) copy-start(f32[7168]{0:T(1024)} %param.10) | copy-start | bytes 86020
  23.0 515.0 %reduce-scatter.2.cloned.1.call-start = ((), (), s32[]{:S(2)}) async-start(), calls=%async_computation.2 | async-start | bytes 15597568 | tf_op jit(solution)/shard_map/reduce_scatter | solution.py:97
  291.4 11.8 %copy-start.3 = (bf16[7168,256]{1,0:T(8,128)(2,1)S(1)}, bf16[7168,256]{1,0:T(8,128)(2,1)}, u32[]{:S(2)}) copy-start(bf16[7168,256]{1,0:T(8,128)(2,1)} %param.14) | copy-start | bytes 11010052
  303.2 10.6 %copy-start = (bf16[256,7168]{1,0:T(8,128)(2,1)S(1)}, bf16[256,7168]{1,0:T(8,128)(2,1)}, u32[]{:S(2)}) copy-start(bf16[256,7168]{1,0:T(8,128)(2,1)} %param.15) | copy-start | bytes 11010052
Sparse Core Ops, SparseCore 0:
  321.2 216.8 reduce-scatter.1
